TPU v7x, 128 devices: a whole 4x4x4 slice. The times are simulated.
128 devices in a mesh: cp: 32 (over z, y, x_lo), fsdp: 4 (over x_hi, core).
Axes of the slice: x: 4 (x_hi: 2, x_lo: 2; x = x_hi * 2 + x_lo), y: 4, z: 4, core: 2. Of those that a mesh axis runs over, the one named last changes fastest.
Arguments:
- query_states: bfloat16 [4, 4096, 1024], P('fsdp', 'cp'), may hold values from -32 to 32
- key_states: bfloat16 [4, 4096, 1024], P('fsdp', 'cp'), may hold values from -32 to 32
- value_states: bfloat16 [4, 4096, 1024], P('fsdp', 'cp'), may hold values from -6 to 6
- span_order: int32 [64], replicated, may hold values from 0 to 63, as said below
- block_mask: int32 [64, 64], replicated, may hold values from 0 to 1, as said below
- output_weight: bfloat16 [1024, 2048], P(('cp', 'fsdp')), may hold values from -0.1875 to 0.1875
- upstream: bfloat16 [4, 4096, 2048], P('fsdp', 'cp'), may hold values from -6 to 6
Outputs:
- projected: bfloat16 [4, 4096, 2048], P('fsdp', 'cp')
- query_gradient: bfloat16 [4, 4096, 1024], P('fsdp', 'cp')
- key_gradient: bfloat16 [4, 4096, 1024], P('fsdp', 'cp')
- value_gradient: bfloat16 [4, 4096, 1024], P('fsdp', 'cp')
- weight_gradient: float32 [1024, 2048], P(('cp', 'fsdp'))
Inputs may be any that keep to these rules, and one draw needn't show every extreme that they name: `span_order`: entries 2 d and 2 d + 1 hold positions p and 63 - p; every position appears once. `block_mask`: the diagonal is 1.
All inputs are finite; a program needn't handle non-finite values.
Results may differ from a plain program's by a relative error of at most 0.024.
Values may be sent and summed in bfloat16 or wider, within the bound.
No kernel may reach another device: no remote copies, remote signals or barrier semaphores. Data moves between devices by JAX's collectives and lax.ppermute only.
A program may use at most 128 MiB of HBM per device.

v0:
```python
import math
import jax
import jax.numpy as jnp
from jax import lax
from jax.sharding import PartitionSpec as P

HEADS = 8
HEAD = 128
lowest = -1e30


def side_by_side(arrays, axis, dim, along):
    widths = [a.shape[along] for a in arrays]
    both = jnp.concatenate(arrays, axis=along)
    filled = lax.all_gather(both, axis, axis=dim, tiled=True)
    return tuple(jnp.split(filled, [sum(widths[:k]) for k in range(1, len(widths))], axis=along))


def cut_along(array, dim, size):
    before, after = (array.shape[:dim], array.shape[dim + 1 :])
    return jnp.moveaxis(array.reshape(*before, size, -1, *after), dim, 0)


def summed_on_arrival(array, axis, dim):
    size = lax.axis_size(axis)
    tiles = lax.all_to_all(cut_along(array, dim, size), axis, 0, 0, tiled=True)
    return jnp.sum(tiles.astype(jnp.float32), axis=0)


def split_heads(row_block):
    return row_block.reshape(row_block.shape[0], HEADS, HEAD)


def pair_scores(query_rows, key_rows):
    return jnp.einsum(
        "qhd,khd->hqk",
        split_heads(query_rows),
        split_heads(key_rows),
        preferred_element_type=jnp.float32,
    ) * (1.0 / HEAD)


def storage_mask(span_order, block_mask):
    span_count = span_order.shape[0]
    onehot = (span_order[:, None] == jnp.arange(span_count, dtype=jnp.int32)[None, :]).astype(
        jnp.float32
    )
    permuted = jnp.dot(jnp.dot(onehot, block_mask.astype(jnp.float32)), onehot.T)
    return permuted > 0.5


def allowed_block(span_ok, positions, query_begin, query_total, key_begin, key_total, span_rows):
    span_sub = lax.dynamic_slice(
        span_ok,
        (query_begin // span_rows, key_begin // span_rows),
        (query_total // span_rows, key_total // span_rows),
    )
    spread = jnp.broadcast_to(
        span_sub[:, None, :, None],
        (query_total // span_rows, span_rows, key_total // span_rows, span_rows),
    )
    spread = spread.reshape(query_total, key_total)
    query_pos = lax.dynamic_slice_in_dim(positions, query_begin, query_total)
    key_pos = lax.dynamic_slice_in_dim(positions, key_begin, key_total)
    return spread & (key_pos[None, :] <= query_pos[:, None])


def local_terms(query_rows, grad_rows, log_rows, delta_rows, key_rows, value_rows, allowed):
    scores = pair_scores(query_rows, key_rows)
    probability = jnp.where(allowed[None], jnp.exp(scores - log_rows[..., None]), 0.0)
    dprob = jnp.einsum(
        "qhd,khd->hqk",
        split_heads(grad_rows),
        split_heads(value_rows),
        preferred_element_type=jnp.float32,
    )
    dscores = (probability * (dprob - delta_rows[..., None]) * (1.0 / HEAD)).astype(jnp.bfloat16)
    return (probability, dscores)


def local(query_states, key_states, value_states, span_order, block_mask, output_weight, upstream):
    query_rows = query_states[0]
    key_local = key_states[0]
    value_local = value_states[0]
    upstream_rows = upstream[0]
    tokens = query_rows.shape[0]
    span_rows = tokens // 2
    positions = (
        span_order[:, None] * span_rows + jnp.arange(span_rows, dtype=jnp.int32)[None, :]
    ).reshape(-1)
    span_ok = storage_mask(span_order, block_mask)
    own_start = lax.axis_index("cp") * tokens
    key_all, value_all = side_by_side((key_local, value_local), "cp", 0, 1)
    weight = lax.all_gather(output_weight, ("cp", "fsdp"), axis=0, tiled=True)
    length = key_all.shape[0]
    key_block = math.gcd(length, 512)
    block_count = length // key_block
    block_steps = jnp.arange(block_count, dtype=jnp.int32)

    def stats_step(running, step_index):
        key_begin = step_index * key_block
        key_rows = lax.dynamic_slice_in_dim(key_all, key_begin, key_block)
        allowed = allowed_block(
            span_ok, positions, own_start, tokens, key_begin, key_block, span_rows
        )
        maxima, totals = running
        scores = pair_scores(query_rows, key_rows)
        masked = jnp.where(allowed[None], scores, lowest)
        new_max = jnp.maximum(maxima, masked.max(-1))
        exp_terms = jnp.where(allowed[None], jnp.exp(scores - new_max[..., None]), 0.0)
        return ((new_max, totals * jnp.exp(maxima - new_max) + exp_terms.sum(-1)), None)

    stat_start = (
        jnp.full((HEADS, tokens), lowest, jnp.float32),
        jnp.zeros((HEADS, tokens), jnp.float32),
    )
    (maxima, totals), _ = lax.scan(stats_step, stat_start, block_steps)
    log_total = maxima + jnp.log(totals)

    def output_step(attn_sum, step_index):
        key_begin = step_index * key_block
        key_rows = lax.dynamic_slice_in_dim(key_all, key_begin, key_block)
        value_rows = lax.dynamic_slice_in_dim(value_all, key_begin, key_block)
        allowed = allowed_block(
            span_ok, positions, own_start, tokens, key_begin, key_block, span_rows
        )
        scores = pair_scores(query_rows, key_rows)
        probability = jnp.where(allowed[None], jnp.exp(scores - log_total[..., None]), 0.0)
        return (
            attn_sum
            + jnp.einsum(
                "hqk,khd->qhd",
                probability.astype(jnp.bfloat16),
                split_heads(value_rows),
                preferred_element_type=jnp.float32,
            ),
            None,
        )

    zero_heads = jnp.zeros((tokens, HEADS, HEAD), jnp.float32)
    attn_sum, _ = lax.scan(output_step, zero_heads, block_steps)
    attended = lax.optimization_barrier(attn_sum.reshape(tokens, -1).astype(jnp.bfloat16))
    projected = jnp.dot(attended, weight, preferred_element_type=jnp.float32).astype(jnp.bfloat16)
    grad_attended = lax.dot_general(
        upstream_rows, weight, (((1,), (1,)), ((), ())), preferred_element_type=jnp.float32
    ).astype(jnp.bfloat16)
    grad_attended = lax.optimization_barrier(grad_attended)
    weight_term = lax.dot_general(
        attended, upstream_rows, (((0,), (0,)), ((), ())), preferred_element_type=jnp.float32
    )
    row_delta = (
        (grad_attended.astype(jnp.float32) * attended.astype(jnp.float32))
        .reshape(tokens, HEADS, HEAD)
        .sum(-1)
    )
    delta_heads = row_delta.T

    def query_step(grad_sum, step_index):
        key_begin = step_index * key_block
        key_rows = lax.dynamic_slice_in_dim(key_all, key_begin, key_block)
        value_rows = lax.dynamic_slice_in_dim(value_all, key_begin, key_block)
        allowed = allowed_block(
            span_ok, positions, own_start, tokens, key_begin, key_block, span_rows
        )
        probability, dscores = local_terms(
            query_rows, grad_attended, log_total, delta_heads, key_rows, value_rows, allowed
        )
        return (
            grad_sum
            + jnp.einsum(
                "hqk,khd->qhd", dscores, split_heads(key_rows), preferred_element_type=jnp.float32
            ),
            None,
        )

    query_sum, _ = lax.scan(query_step, zero_heads, block_steps)
    query_gradient = query_sum.reshape(tokens, -1).astype(jnp.bfloat16)
    log_all, delta_all = side_by_side((log_total.T, row_delta), "cp", 0, 1)
    sums_now = (zero_heads, zero_heads)
    query_piece, grad_piece = side_by_side((query_rows, grad_attended), "cp", 0, 1)
    row_count = query_piece.shape[0]
    sources = row_count // tokens
    group_size = math.gcd(sources, max(1, 512 // tokens))
    group_rows = group_size * tokens

    def group_step(running, step_index):
        offset = step_index * group_rows
        query_group = lax.dynamic_slice_in_dim(query_piece, offset, group_rows)
        grad_group = lax.dynamic_slice_in_dim(grad_piece, offset, group_rows)
        log_group = lax.dynamic_slice_in_dim(log_all, offset, group_rows).T
        delta_group = lax.dynamic_slice_in_dim(delta_all, offset, group_rows).T
        allowed = allowed_block(
            span_ok, positions, offset, group_rows, own_start, tokens, span_rows
        )
        key_sum, value_sum = running
        probability, dscores = local_terms(
            query_group, grad_group, log_group, delta_group, key_local, value_local, allowed
        )
        probability_low = probability.astype(jnp.bfloat16).reshape(
            HEADS, group_size, tokens, tokens
        )
        dscores_group = dscores.reshape(HEADS, group_size, tokens, tokens)
        qsplit = query_group.reshape(group_size, tokens, HEADS, HEAD)
        gsplit = grad_group.reshape(group_size, tokens, HEADS, HEAD)
        key_part = jnp.einsum(
            "hgqk,gqhd->gkhd", dscores_group, qsplit, preferred_element_type=jnp.float32
        ).astype(jnp.bfloat16)
        value_part = jnp.einsum(
            "hgqk,gqhd->gkhd", probability_low, gsplit, preferred_element_type=jnp.float32
        ).astype(jnp.bfloat16)
        key_part, value_part = lax.optimization_barrier((key_part, value_part))
        return (
            (
                key_sum + key_part.astype(jnp.float32).sum(0),
                value_sum + value_part.astype(jnp.float32).sum(0),
            ),
            None,
        )

    sums_now, _ = lax.scan(group_step, sums_now, jnp.arange(sources // group_size, dtype=jnp.int32))
    key_sum, value_sum = sums_now
    key_gradient = key_sum.reshape(tokens, -1).astype(jnp.bfloat16)
    value_gradient = value_sum.reshape(tokens, -1).astype(jnp.bfloat16)
    cycle_count = lax.axis_size("cp")
    batch_count = lax.axis_size("fsdp")
    slab_rows = weight_term.shape[0] // (cycle_count * batch_count)
    reordered = weight_term.reshape(cycle_count, batch_count, slab_rows, -1).transpose(1, 0, 2, 3)
    reordered = reordered.reshape(weight_term.shape[0], -1)
    partial_batch = summed_on_arrival(reordered.astype(jnp.bfloat16), "fsdp", 0)
    weight_gradient = summed_on_arrival(partial_batch.astype(jnp.bfloat16), "cp", 0)
    return (
        projected[None],
        query_gradient[None],
        key_gradient[None],
        value_gradient[None],
        weight_gradient,
    )


def solution(mesh):
    return jax.shard_map(
        local,
        mesh=mesh,
        in_specs=(
            P("fsdp", "cp", None),
            P("fsdp", "cp", None),
            P("fsdp", "cp", None),
            P(),
            P(),
            P(("cp", "fsdp"), None),
            P("fsdp", "cp", None),
        ),
        out_specs=(
            P("fsdp", "cp", None),
            P("fsdp", "cp", None),
            P("fsdp", "cp", None),
            P("fsdp", "cp", None),
            P(("cp", "fsdp"), None),
        ),
        check_vma=False,
    )
```

profile of v0, /device:TPU:1, one launch (start us, length us, event | category | flops | bytes accessed | tf_op | source)
XLA Modules:
  0.0 1168.4 jit_solution(7732555768528166424)
XLA Ops:
  11.1 199.5 %all-gather.6.cloned.1.call-done = bf16[1024,2048]{1,0:T(8,128)(2,1)} async-done(((bf16[8,2048]{1,0:T(8,128)(2,1)}), bf16[1024,2048]{1,0:T(8,128)(2,1)}) %all-gather.6.cloned.1.call-update) | async-done | bytes 4194320 | tf_op jit(solution)/shard_map/all_gather | solution.py:94
  210.6 3.7 convolution_convert_fusion.3
  215.9 354.4 %all-gather.4.cloned.1.call-done = bf16[4096,2048]{0,1:T(8,128)(2,1)} async-done(((bf16[128,2048]{0,1:T(8,128)(2,1)}), bf16[4096,2048]{0,1:T(8,128)(2,1)}) %all-gather.4.cloned.1.call-update) | async-done | bytes 16777232 | tf_op jit(solution)/shard_map/all_gather | solution.py:15
  570.3 11.8 %fusion.61 = (bf16[4096,1024]{0,1:T(8,128)(2,1)}, bf16[4096,1024]{0,1:T(8,128)(2,1)}) fusion(bf16[4096,2048]{0,1:T(8,128)(2,1)} %all-gather.4.cloned.1.call-done), kind=kLoop, calls=%fused_computation.94 | loop fusion | bytes 33554432 | tf_op jit(solution)/shard_map/split | solution.py:16
  582.1 36.4 %while.60 = (s32[]{:T(128)}, f32[8,128]{1,0:T(8,128)S(1)}, f32[8,128]{1,0:T(8,128)S(1)}, s32[8]{0:T(128)S(1)}, pred[64,64]{1,0:T(8,128)(4,1)S(1)}, /*index=5*/s3...) while((s32[]{:T(128)}, f32[8,128]{1,0:T(8,128)S(1)}, ...), condition=%wide.region_3.4_spmd.clone, body=%wide.region_0.3_spmd.clone.sunk | while | flops 138023952 | bytes 8776669 | solution.py:117
  618.5 51.7 %while.61 = (s32[]{:T(128)}, f32[128,8,128]{0,2,1:T(8,128)}, s32[8]{0:T(128)S(1)}, bf16[4096,1024]{0,1:T(8,128)(2,1)}, pred[64,64]{1,0:T(8,128)(4,1)S(1)}, /*ind...) while((s32[]{:T(128)}, f32[128,8,128]{0,2,1:T(8,128)}, ...), condition=%wide.region_5.6_spmd.clone, body=%wide.region_4.5_spmd.clone.sunk | while | flops 270925856 | bytes 8661988 | solution.py:141
  619.8 1.7 constant_dynamic-slice_fusion.13
  622.3 1.7 fusion.109
  625.3 1.7 constant_dynamic-slice_fusion.13
  627.9 2.8 fusion.109
  631.9 1.7 constant_dynamic-slice_fusion.13
  634.5 2.8 fusion.109
  638.5 1.7 constant_dynamic-slice_fusion.13
  641.1 2.8 fusion.109
  645.1 1.7 constant_dynamic-slice_fusion.13
  647.7 2.8 fusion.109
  651.7 1.7 constant_dynamic-slice_fusion.13
  654.3 2.8 fusion.109
  660.9 2.8 fusion.109
  667.5 2.8 fusion.109
  673.3 2.3 copy.258
  675.6 5.5 all-to-all-start
  681.2 75.2 %while.62 = (s32[]{:T(128)}, f32[128,8,128]{0,2,1:T(8,128)}, s32[8]{0:T(128)S(1)}, bf16[4096,1024]{0,1:T(8,128)(2,1)}, pred[64,64]{1,0:T(8,128)(4,1)S(1)}, /*ind...) while((s32[]{:T(128)}, f32[128,8,128]{0,2,1:T(8,128)}, ...), condition=%wide.region_8.9_spmd.clone, body=%wide.region_7.8_spmd.clone.sunk | while | flops 406716416 | bytes 14171124 | solution.py:176
  682.4 1.7 constant_dynamic-slice_fusion.14
  684.2 1.9 fusion.116
  686.9 3.6 fusion.117
  693.5 1.9 fusion.116
  696.2 3.7 fusion.117
  702.9 1.9 fusion.116
  705.6 3.7 fusion.117
  712.3 1.9 fusion.116
  715.0 3.7 fusion.117
  721.7 1.9 fusion.116
  724.4 3.7 fusion.117
  731.1 1.9 fusion.116
  733.8 3.7 fusion.117
  740.5 1.9 fusion.116
  743.2 3.7 fusion.117
  749.9 1.9 fusion.116
  752.6 3.7 fusion.117
  758.3 3.7 fusion.46
  762.0 13.3 %all-to-all-done = bf16[4,256,2048]{2,1,0:T(8,128)(2,1)} async-done(((bf16[4,256,2048]{2,1,0:T(8,128)(2,1)}), bf16[4,256,2048]{2,1,0:T(8,128)(2,1)}, u32[]{:S(2)}, u32[]{:S(2)}) %all-to-all-start) | async-done | bytes 4194336 | tf_op jit(solution)/shard_map/all_to_all | solution.py:26
  775.3 4.3 reduce_sum.70
  779.5 7.7 all-to-all-start.1
  787.3 94.1 %all_gather.15 = f32[4096,16]{0,1:T(8,128)S(1)} all-gather(f32[128,16]{0,1:T(8,128)S(1)} %pad_maximum_fusion.2), channel_id=1, replica_groups=mesh['cp'=32,'fsdp'=4] {'cp'}, dimensions={0}, use_global_device_ids=true | all-gather | bytes 270336 | tf_op jit(solution)/shard_map/all_gather | solution.py:15
  882.9 115.3 %all-gather.8.cloned.1.call-done = bf16[4096,2048]{1,0:T(8,128)(2,1)} async-done(((bf16[128,2048]{1,0:T(8,128)(2,1)}), bf16[4096,2048]{1,0:T(8,128)(2,1)}) %all-gather.8.cloned.1.call-update) | async-done | bytes 16777232 | tf_op jit(solution)/shard_map/all_gather | solution.py:15
  998.1 11.6 fusion.60
  1009.8 148.1 %while.63 = (s32[]{:T(128)}, f32[128,8,128]{0,2,1:T(8,128)}, f32[128,8,128]{0,2,1:T(8,128)}, s32[8]{0:T(128)S(1)}, bf16[4096,1024]{1,0:T(8,128)(2,1)}, /*index=5...) while((s32[]{:T(128)}, f32[128,8,128]{0,2,1:T(8,128)}, ...), condition=%wide.region_12.13_spmd.clone, body=%wide.region_9.12_spmd.clone.sunk | while | flops 544604160 | bytes 55680292 | solution.py:220
  1014.8 1.9 fusion.125
  1016.7 2.3 constant_dynamic-slice_fusion.16
  1033.4 1.9 fusion.125
  1035.2 2.3 constant_dynamic-slice_fusion.16
  1051.9 1.9 fusion.125
  1053.7 2.3 constant_dynamic-slice_fusion.16
  1070.4 1.9 fusion.125
  1072.3 2.3 constant_dynamic-slice_fusion.16
  1088.9 1.9 fusion.125
  1090.8 2.3 constant_dynamic-slice_fusion.16
  1107.4 1.9 fusion.125
  1109.3 2.3 constant_dynamic-slice_fusion.16
  1125.9 1.9 fusion.125
  1127.8 2.3 constant_dynamic-slice_fusion.16
  1144.4 1.9 fusion.125
  1146.3 2.3 constant_dynamic-slice_fusion.16
  (643 shorter events, 192.2 us)
Async XLA Ops:
  7.2 203.4 %copy-start = (bf16[1,128,2048]{2,1,0:T(8,128)(2,1)S(1)}, bf16[1,128,2048]{2,1,0:T(8,128)(2,1)}, u32[]{:S(2)}) copy-start(bf16[1,128,2048]{2,1,0:T(8,128)(2,1)} %param.21) | copy-start | bytes 1572868
  7.2 203.4 %all-gather.6.cloned.1.call-start = ((), (), s32[]{:S(2)}) async-start(), calls=%async_computation.3 | async-start | bytes 4227072 | tf_op jit(solution)/shard_map/all_gather | solution.py:94
  7.9 562.4 %all-gather.4.cloned.1.call-start = ((), (), s32[]{:S(2)}) async-start(), calls=%async_computation.2 | async-start | bytes 17301504 | tf_op jit(solution)/shard_map/all_gather | solution.py:15
  11.1 203.3 %copy-start.4 = (bf16[1,128,1024]{2,1,0:T(8,128)(2,1)S(1)}, bf16[1,128,1024]{2,1,0:T(8,128)(2,1)}, u32[]{:S(2)}) copy-start(bf16[1,128,1024]{2,1,0:T(8,128)(2,1)} %param.15) | copy-start | bytes 786436
  11.1 204.2 %copy-start.15 = (s32[64]{0:T(128)S(1)}, s32[64]{0:T(128)}, u32[]{:S(2)}) copy-start(s32[64]{0:T(128)} %param.18) | copy-start | bytes 772
  11.1 204.3 %copy-start.14 = (s32[64,64]{1,0:T(8,128)S(1)}, s32[64,64]{1,0:T(8,128)}, u32[]{:S(2)}) copy-start(s32[64,64]{1,0:T(8,128)} %param.19) | copy-start | bytes 49156
  11.1 987.0 %all-gather.8.cloned.1.call-start = ((), (), s32[]{:S(2)}) async-start(), calls=%async_computation.4 | async-start | bytes 17301504 | tf_op jit(solution)/shard_map/all_gather | solution.py:15
  675.6 99.6 %all-to-all-start = ((bf16[4,256,2048]{2,1,0:T(8,128)(2,1)}), bf16[4,256,2048]{2,1,0:T(8,128)(2,1)}, u32[]{:S(2)}, u32[]{:S(2)}) async-start(bf16[4,256,2048]{2,1,0:T(8,128)(2,1)} %bitcast.259), calls=%async_computation | async-start | bytes 8388608 | tf_op jit(solution)/shard_map/all_to_all | solution.py:26
  779.5 102.5 %all-to-all-start.1 = ((bf16[32,8,2048]{2,1,0:T(8,128)(2,1)}), bf16[32,8,2048]{2,1,0:T(8,128)(2,1)S(1)}, u32[]{:S(2)}, u32[]{:S(2)}) async-start(bf16[32,8,2048]{2,1,0:T(8,128)(2,1)} %bitcast.17), calls=%async_computation.1 | async-start | bytes 2097152 | tf_op jit(solution)/shard_map/all_to_all | solution.py:26
  882.9 126.9 %copy-start.10 = (bf16[1,128,1024]{2,1,0:T(8,128)(2,1)S(1)}, bf16[1,128,1024]{2,1,0:T(8,128)(2,1)}, u32[]{:S(2)}) copy-start(bf16[1,128,1024]{2,1,0:T(8,128)(2,1)} %param.16) | copy-start | bytes 786436
  1009.8 4.2 copy-start.12
  1016.7 4.5 copy-start.9
  1021.3 1.2 copy-start.3
  1022.5 1.6 copy-start.2
  1025.8 1.2 copy-start.7
  1026.1 2.2 copy-start.11
  1026.1 2.2 copy-start.13
  1028.3 4.1 copy-start.12
  1035.2 4.5 copy-start.9
  1039.8 1.2 copy-start.3
  1041.1 1.6 copy-start.2
  1044.3 1.2 copy-start.7
  1044.6 2.2 copy-start.11
  1044.7 2.2 copy-start.13
  1046.8 4.1 copy-start.12
  1053.7 4.5 copy-start.9
  1058.3 1.2 copy-start.3
  1059.6 1.6 copy-start.2
  1062.8 1.2 copy-start.7
  1063.1 2.2 copy-start.11
  1063.2 2.2 copy-start.13
  1065.4 4.1 copy-start.12
  1072.3 4.5 copy-start.9
  1076.9 1.2 copy-start.3
  1078.1 1.6 copy-start.2
  1081.3 1.2 copy-start.7
  1081.7 2.2 copy-start.11
  1081.7 2.2 copy-start.13
  1083.9 4.1 copy-start.12
  1090.8 4.5 copy-start.9
  1095.4 1.2 copy-start.3
  1096.6 1.6 copy-start.2
  1100.2 2.2 copy-start.11
  1100.2 2.2 copy-start.13
  1102.4 4.1 copy-start.12
  1109.3 4.5 copy-start.9
  1113.9 1.2 copy-start.3
  1115.1 1.6 copy-start.2
  1118.7 2.2 copy-start.11
  1118.7 2.2 copy-start.13
  1120.9 4.1 copy-start.12
  1127.8 4.5 copy-start.9
  1132.4 1.2 copy-start.3
  1133.6 1.6 copy-start.2
  1136.8 1.2 copy-start.7
  1137.2 2.2 copy-start.11
  1137.2 2.2 copy-start.13
  1139.4 4.1 copy-start.12
  1146.3 4.5 copy-start.9
  1150.9 1.2 copy-start.3
  1152.1 1.6 copy-start.2
  1155.7 2.2 copy-start.11
  1155.7 2.2 copy-start.13
  1157.9 3.9 copy-start.1
  (27 other events, 26.1 us)
Sparse Core Ops, SparseCore 0:
  9.7 200.8 all-gather.5
  212.2 358.1 all-gather.3
  572.0 426.1 all-gather.7
where the time goes:
time: 1170 us
  waiting for transfers between devices  683 us (58%)
  local copies, waits for them, and re-layouts  196 us (17%)
  matrix products  119 us (10%)
  blocking collectives  94.1 us (8%)
  other arithmetic  24.1 us (2%)
  loops' own time  23.7 us (2%)
  between operations  14 us (1%)
  starting transfers between devices  13.4 us (1%)
    all_gather x2, waiting for transfers between devices, side_by_side(): filled = lax.all_gather(both, axis, axis=dim, tiled=True)  470 us
    all_gather x1, waiting for transfers between devices, local(): weight = lax.all_gather(output_weight, ('cp', 'fsdp'), axis=0, tiled=True)  199 us
    all_gather x1, blocking collectives, side_by_side(): filled = lax.all_gather(both, axis, axis=dim, tiled=True)  94.1 us
    dot_general x24, matrix products, pair_scores(): jnp.einsum('qhd,khd->hqk', split_heads(query_rows), split_heads(key_rows)...  34.9 us
    dynamic_slice x16, local copies, waits for them, and re-layouts, group_step(): grad_group = lax.dynamic_slice_in_dim(grad_piece, offset, group_rows)  30.5 us
    dot_general x8, matrix products, query_step(): jnp.einsum('hqk,khd->qhd', dscores, split_heads(key_rows), preferred_elem...  29.7 us
    split x3, local copies, waits for them, and re-layouts, side_by_side(): jnp.split(filled, [sum(widths[:k]) for k in range(1, len(widths))], axis=...  24.1 us
  transfers between devices with their start and end apart: 5, of which 4 were waited for; matrix products, arithmetic and copies ran while one was open for 16% of the time, Pallas kernels for 0%

commit v1 on v0

--- a/solution.py
+++ b/solution.py
@@ -91,7 +91,12 @@
     span_ok = storage_mask(span_order, block_mask)
     own_start = lax.axis_index("cp") * tokens
     key_all, value_all = side_by_side((key_local, value_local), "cp", 0, 1)
-    weight = lax.all_gather(output_weight, ("cp", "fsdp"), axis=0, tiled=True)
+    weight = jnp.concatenate(
+        lax.all_to_all(
+            jnp.stack([output_weight] * lax.axis_size(("cp", "fsdp"))), ("cp", "fsdp"), 0, 0
+        ),
+        axis=0,
+    )
     length = key_all.shape[0]
     key_block = math.gcd(length, 512)
     block_count = length // key_block

time: 1170 us -> 1020 us (0.87)
  waiting for transfers between devices: 683 us -> 420 us
  blocking collectives: 94.1 us -> 187 us
  local copies, waits for them, and re-layouts: 196 us -> 227 us
  matrix products: 119 us -> 96.2 us
    all_gather x1 -> x0, waiting for transfers between devices: 199 us -> none  [local(): weight = lax.all_gather(output_weight, ('cp', 'fsdp'), axis=0, tiled=True)]
    all_to_all x0 -> x1, blocking collectives: none -> 109 us  [local(): lax.all_to_all(jnp.stack([output_weight] * lax.axis_size(('cp', 'fsdp')))...]
    all_gather x2, waiting for transfers between devices: 470 us -> 420 us  [side_by_side(): filled = lax.all_gather(both, axis, axis=dim, tiled=True)]
    all_gather x1, blocking collectives: 94.1 us -> 77.4 us  [side_by_side(): filled = lax.all_gather(both, axis, axis=dim, tiled=True)]
    dynamic_slice x24, local copies, waits for them, and re-layouts: 1.9 us -> 18.2 us  [allowed_block(): key_pos = lax.dynamic_slice_in_dim(positions, key_begin, key_total)]
    dynamic_slice x16, local copies, waits for them, and re-layouts: 30.5 us -> 14.8 us  [group_step(): grad_group = lax.dynamic_slice_in_dim(grad_piece, offset, group_rows)]
    all_to_all x2, waiting for transfers between devices: 13.3 us -> 0.01 us  [summed_on_arrival(): tiles = lax.all_to_all(cut_along(array, dim, size), axis, 0, 0, tiled=True)]
    while x208, local copies, waits for them, and re-layouts: 17.8 us -> 30.7 us
  transfers between devices with their start and end apart: 5 -> 4, of which waited for: 4 -> 2; matrix products, arithmetic and copies ran while one was open for 16% -> 32% of each run, Pallas kernels for 0% -> 0%
where the time goes in v1:
time: 1020 us; the launch traced here: 1010 us
  waiting for transfers between devices  420 us (41%)
  local copies, waits for them, and re-layouts  227 us (22%)
  blocking collectives  187 us (18%)
  matrix products  96.2 us (9%)
  other arithmetic  27.4 us (3%)
  loops' own time  24.7 us (2%)
  between operations  14.3 us (1%)
  starting transfers between devices  13.2 us (1%)
    all_gather x2, waiting for transfers between devices, side_by_side(): filled = lax.all_gather(both, axis, axis=dim, tiled=True)  420 us
    all_to_all x1, blocking collectives, local(): lax.all_to_all(jnp.stack([output_weight] * lax.axis_size(('cp', 'fsdp')))...  109 us
    all_gather x1, blocking collectives, side_by_side(): filled = lax.all_gather(both, axis, axis=dim, tiled=True)  77.4 us
    while x208, local copies, waits for them, and re-layouts  30.7 us
    dot_general x8, matrix products, query_step(): jnp.einsum('hqk,khd->qhd', dscores, split_heads(key_rows), preferred_elem...  27.8 us
    dynamic_slice x32, local copies, waits for them, and re-layouts, local(): (maxima, totals), _ = lax.scan(stats_step, stat_start, block_steps)  24.7 us
    dot_general x24, matrix products, pair_scores(): jnp.einsum('qhd,khd->hqk', split_heads(query_rows), split_heads(key_rows)...  23.9 us
    split x3, local copies, waits for them, and re-layouts, side_by_side(): jnp.split(filled, [sum(widths[:k]) for k in range(1, len(widths))], axis=...  23.4 us
  transfers between devices with their start and end apart: 4, of which 2 were waited for; matrix products, arithmetic and copies ran while one was open for 32% of the time, Pallas kernels for 0%

profile of v1, /device:TPU:1, one launch (start us, length us, event | category | flops | bytes accessed | tf_op | source)
XLA Modules:
  0.0 1010.1 jit_solution(11107434240295839737)
XLA Ops:
  11.0 109.1 %all_to_all.15 = bf16[128,8,2048]{2,1,0:T(8,128)(2,1)S(1)} all-to-all(bf16[128,8,2048]{2,1,0:T(8,128)(2,1)S(1)} %stack.2), channel_id=1, replica_groups=mesh['cp'=32,'fsdp'=4] {'cp','fsdp'}, dimensions={0} | all-to-all | bytes 8388608 | tf_op jit(solution)/shard_map/all_to_all | solution.py:95
  120.1 2.1 copy-done.4
  122.2 2.2 fusion.56
  124.4 1.8 pad_maximum_fusion.1
  128.8 290.5 %all-gather.3.cloned.1.call-done = bf16[4096,2048]{0,1:T(8,128)(2,1)} async-done(((bf16[128,2048]{0,1:T(8,128)(2,1)}), bf16[4096,2048]{0,1:T(8,128)(2,1)}) %all-gather.3.cloned.1.call-update) | async-done | bytes 16777232 | tf_op jit(solution)/shard_map/all_gather | solution.py:15
  419.3 11.7 %fusion.73 = (bf16[4096,1024]{0,1:T(8,128)(2,1)}, bf16[4096,1024]{0,1:T(8,128)(2,1)}) fusion(bf16[4096,2048]{0,1:T(8,128)(2,1)} %all-gather.3.cloned.1.call-done), kind=kLoop, calls=%fused_computation.98 | loop fusion | bytes 33554432 | tf_op jit(solution)/shard_map/split | solution.py:16
  431.0 42.7 %while.60 = (s32[]{:T(128)}, f32[8,128]{1,0:T(8,128)S(1)}, f32[8,128]{1,0:T(8,128)S(1)}, s32[8]{0:T(128)S(1)}, pred[64,64]{1,0:T(8,128)(4,1)S(1)}, /*index=5*/s3...) while((s32[]{:T(128)}, f32[8,128]{1,0:T(8,128)S(1)}, ...), condition=%wide.region_3.4_spmd.clone, body=%wide.region_0.3_spmd.clone.sunk | while | flops 138023952 | bytes 8776669 | solution.py:122
  473.8 57.1 %while.61 = (s32[]{:T(128)}, f32[128,8,128]{0,2,1:T(8,128)}, s32[8]{0:T(128)S(1)}, bf16[4096,1024]{0,1:T(8,128)(2,1)}, pred[64,64]{1,0:T(8,128)(4,1)S(1)}, /*ind...) while((s32[]{:T(128)}, f32[128,8,128]{0,2,1:T(8,128)}, ...), condition=%wide.region_5.6_spmd.clone, body=%wide.region_4.5_spmd.clone.sunk | while | flops 270925856 | bytes 8661988 | solution.py:146
  476.6 1.7 constant_dynamic-slice_fusion.13
  478.3 1.7 fusion.119
  484.5 2.8 fusion.119
  490.1 1.7 constant_dynamic-slice_fusion.13
  491.8 2.8 fusion.119
  499.0 2.8 fusion.119
  504.6 1.7 constant_dynamic-slice_fusion.13
  506.3 2.8 fusion.119
  511.8 1.7 constant_dynamic-slice_fusion.13
  513.5 2.8 fusion.119
  520.8 2.8 fusion.119
  526.3 1.7 constant_dynamic-slice_fusion.13
  528.1 2.8 fusion.119
  533.5 2.3 copy.258
  535.8 8.5 all-to-all-start.1
  546.8 81.7 %while.62 = (s32[]{:T(128)}, f32[128,8,128]{0,2,1:T(8,128)}, s32[8]{0:T(128)}, bf16[4096,1024]{0,1:T(8,128)(2,1)}, pred[64,64]{1,0:T(8,128)(4,1)S(1)}, /*index=5...) while((s32[]{:T(128)}, f32[128,8,128]{0,2,1:T(8,128)}, ...), condition=%wide.region_8.9_spmd.clone, body=%wide.region_7.8_spmd.clone.sunk | while | flops 406716416 | bytes 14171124 | solution.py:181
  550.2 2.8 constant_dynamic-slice_fusion.14
  553.5 3.4 fusion.127
  560.3 2.8 constant_dynamic-slice_fusion.14
  563.6 3.5 fusion.127
  570.6 2.8 constant_dynamic-slice_fusion.14
  573.9 3.5 fusion.127
  580.8 2.8 constant_dynamic-slice_fusion.14
  584.1 3.5 fusion.127
  591.1 2.8 constant_dynamic-slice_fusion.14
  594.3 3.5 fusion.127
  601.3 2.8 constant_dynamic-slice_fusion.14
  604.6 3.5 fusion.127
  611.5 2.8 constant_dynamic-slice_fusion.14
  614.8 3.5 fusion.127
  621.8 2.8 constant_dynamic-slice_fusion.14
  625.0 3.5 fusion.127
  630.5 77.4 %all_gather.11 = f32[4096,16]{0,1:T(8,128)S(1)} all-gather(f32[128,16]{0,1:T(8,128)S(1)} %pad_maximum_fusion.2), channel_id=1, replica_groups=mesh['cp'=32,'fsdp'=4] {'cp'}, dimensions={0}, use_global_device_ids=true | all-gather | bytes 270336 | tf_op jit(solution)/shard_map/all_gather | solution.py:15
  708.0 3.8 fusion.53
  711.9 4.3 reduce_sum.70
  716.2 4.7 all-to-all-start.2
  720.9 129.7 %all-gather.5.cloned.1.call-done = bf16[4096,2048]{1,0:T(8,128)(2,1)} async-done(((bf16[128,2048]{1,0:T(8,128)(2,1)}), bf16[4096,2048]{1,0:T(8,128)(2,1)}) %all-gather.5.cloned.1.call-update) | async-done | bytes 16777232 | tf_op jit(solution)/shard_map/all_gather | solution.py:15
  850.5 11.6 %fusion.72 = (bf16[4096,1024]{1,0:T(8,128)(2,1)}, bf16[4096,1024]{1,0:T(8,128)(2,1)}) fusion(bf16[4096,2048]{1,0:T(8,128)(2,1)} %all-gather.5.cloned.1.call-done), kind=kLoop, calls=%fused_computation.97 | loop fusion | bytes 33554432 | tf_op jit(solution)/shard_map/split | solution.py:16
  862.2 135.2 %while.63 = (s32[]{:T(128)}, f32[128,8,128]{0,2,1:T(8,128)}, f32[128,8,128]{0,2,1:T(8,128)}, s32[8]{0:T(128)S(1)}, bf16[4096,1024]{1,0:T(8,128)(2,1)}, /*index=5...) while((s32[]{:T(128)}, f32[128,8,128]{0,2,1:T(8,128)}, ...), condition=%wide.region_12.13_spmd.clone, body=%wide.region_9.12_spmd.clone.sunk | while | flops 544604160 | bytes 51485988 | solution.py:225
  865.6 1.7 copy.297
  872.5 1.9 fusion.135
  882.5 1.7 copy.297
  889.4 1.9 fusion.135
  899.4 1.7 copy.297
  906.3 1.9 fusion.135
  916.3 1.7 copy.297
  923.1 1.9 fusion.135
  933.2 1.7 copy.297
  940.0 1.9 fusion.135
  950.0 1.7 copy.297
  956.9 1.9 fusion.135
  966.9 1.7 copy.297
  973.8 1.9 fusion.135
  983.8 1.7 copy.297
  990.7 1.9 fusion.135
  1001.3 2.0 convert_reduce_fusion.2
  (648 shorter events, 201.1 us)
Async XLA Ops:
  7.2 115.0 %copy-start = (bf16[1,128,2048]{2,1,0:T(8,128)(2,1)S(1)}, bf16[1,128,2048]{2,1,0:T(8,128)(2,1)}, u32[]{:S(2)}) copy-start(bf16[1,128,2048]{2,1,0:T(8,128)(2,1)} %param.21) | copy-start | bytes 1572868
  7.2 3.3 copy-start.16
  7.2 412.1 %all-gather.3.cloned.1.call-start = ((), (), s32[]{:S(2)}) async-start(), calls=%async_computation.3 | async-start | bytes 17301504 | tf_op jit(solution)/shard_map/all_gather | solution.py:15
  10.4 840.1 %all-gather.5.cloned.1.call-start = ((), (), s32[]{:S(2)}) async-start(), calls=%async_computation.4 | async-start | bytes 17301504 | tf_op jit(solution)/shard_map/all_gather | solution.py:15
  120.1 2.1 copy-start.4
  122.1 2.2 copy-start.3
  122.1 4.1 copy-start.17
  122.1 4.1 copy-start.18
  532.1 12.2 %copy-start.11 = (bf16[128,1024]{1,0:T(8,128)(2,1)}, bf16[128,1024]{1,0:T(8,128)(2,1)S(1)}, u32[]{:S(2)}) copy-start(bf16[128,1024]{1,0:T(8,128)(2,1)S(1)} %copy.212) | copy-start | bytes 786436
  535.8 176.1 %all-to-all-start.1 = ((bf16[4,256,2048]{2,1,0:T(8,128)(2,1)}), bf16[4,256,2048]{2,1,0:T(8,128)(2,1)}, u32[]{:S(2)}, u32[]{:S(2)}) async-start(bf16[4,256,2048]{2,1,0:T(8,128)(2,1)} %bitcast.268), calls=%async_computation.1 | async-start | bytes 8388608 | tf_op jit(solution)/shard_map/all_to_all | solution.py:26
  716.2 285.1 %all-to-all-start.2 = ((bf16[32,8,2048]{2,1,0:T(8,128)(2,1)}), bf16[32,8,2048]{2,1,0:T(8,128)(2,1)}, u32[]{:S(2)}, u32[]{:S(2)}) async-start(bf16[32,8,2048]{2,1,0:T(8,128)(2,1)} %bitcast.18), calls=%async_computation.2 | async-start | bytes 2097152 | tf_op jit(solution)/shard_map/all_to_all | solution.py:26
  720.8 141.3 %copy-start.9 = (bf16[1,128,1024]{2,1,0:T(8,128)(2,1)S(1)}, bf16[1,128,1024]{2,1,0:T(8,128)(2,1)}, u32[]{:S(2)}) copy-start(bf16[1,128,1024]{2,1,0:T(8,128)(2,1)} %param.17) | copy-start | bytes 786436
  862.2 2.8 copy-start.12
  862.2 2.8 copy-start.14
  874.4 1.2 copy-start.2
  876.6 1.2 copy-start.7
  876.7 2.3 copy-start.10
  876.7 2.3 copy-start.13
  876.8 2.3 copy-start.15
  879.1 2.8 copy-start.12
  879.1 2.8 copy-start.14
  891.3 1.2 copy-start.2
  893.4 1.2 copy-start.7
  893.6 2.3 copy-start.10
  893.6 2.3 copy-start.13
  893.6 2.3 copy-start.15
  896.0 2.8 copy-start.12
  896.0 2.8 copy-start.14
  908.1 1.2 copy-start.2
  910.3 1.2 copy-start.7
  910.5 2.3 copy-start.10
  910.5 2.3 copy-start.13
  910.5 2.3 copy-start.15
  912.9 2.8 copy-start.12
  912.9 2.8 copy-start.14
  925.0 1.2 copy-start.2
  927.4 2.3 copy-start.10
  927.4 2.3 copy-start.13
  927.4 2.3 copy-start.15
  929.8 2.8 copy-start.12
  929.8 2.8 copy-start.14
  941.9 1.2 copy-start.2
  944.3 2.3 copy-start.10
  944.3 2.3 copy-start.13
  944.3 2.3 copy-start.15
  946.6 2.8 copy-start.12
  946.7 2.8 copy-start.14
  958.8 1.2 copy-start.2
  961.2 2.3 copy-start.10
  961.2 2.3 copy-start.13
  961.2 2.3 copy-start.15
  963.5 2.8 copy-start.12
  963.5 2.8 copy-start.14
  975.7 1.2 copy-start.2
  978.1 2.3 copy-start.10
  978.1 2.3 copy-start.13
  978.1 2.3 copy-start.15
  980.4 2.8 copy-start.12
  980.4 2.8 copy-start.14
  992.6 1.2 copy-start.2
  995.0 2.3 copy-start.10
  995.0 2.3 copy-start.13
  995.0 2.3 copy-start.15
  997.3 6.0 copy-start.1
  (29 other events, 28.6 us)
Sparse Core Ops, SparseCore 0:
  10.5 408.7 all-gather.2
  421.0 429.5 all-gather.4
